TPU v7x, 256 devices: a whole 4x4x8 slice. The times are simulated.
256 devices in a mesh: probe: 4 (over x), space: 64 (over y, z, core).
Axes of the slice: x: 4, y: 4, z: 8, core: 2. Of those that a mesh axis runs over, the one named last changes fastest.
Arguments:
- courant_field: float32 [128, 32, 256], P('space'), may hold values from 0.05 to 0.3
- probe_fields: float32 [16, 128, 32, 256], P('probe', 'space'), may hold values from -6 to 6
- prior_weight: float32 [128, 32, 256], P('space'), may hold values from 0.5 to 5
- source_cells: int32 [4096], P('space'), may hold values from 0 to 1048575, as said below
- source_strength: float32 [4096], P('space'), may hold values from -6 to 6
- wavelet: float32 [8], replicated, may hold values from -4 to 4
- receiver_cells: int32 [4096], P('space'), may hold values from 0 to 1048575, as said below
- receiver_weight: float32 [4096], P('space'), may hold values from 1 to 10
Outputs:
- hessian_fields: float32 [16, 128, 32, 256], P('probe', 'space')
- basis: float32 [16, 128, 32, 256], P('probe', 'space')
Inputs may be any that keep to these rules, and one draw needn't show every extreme that they name: `source_cells`: entries k * 64 to (k + 1) * 64 - 1 are cells of the k-th slab of 2 planes along the first dimension; cells may repeat. `receiver_cells`: entries k * 64 to (k + 1) * 64 - 1 are cells of the k-th slab of 2 planes along the first dimension; cells may repeat.
All inputs are finite; a program needn't handle non-finite values.
Results may differ from a plain program's by a relative error of at most 0.0019.
Values sent between devices are 32-bit elements; how exact they have to be, the bound alone decides.
No kernel may reach another device: no remote copies, remote signals or barrier semaphores. Data moves between devices by JAX's collectives and lax.ppermute only.
A program may use at most 64 MiB of HBM per device.

v0:
```python
import jax
import jax.numpy as jnp
from jax import lax
from jax.sharding import PartitionSpec as P


def extended(block, sides, width):
    for axis, dim in sides:
        count = lax.axis_size(axis)
        forward = [(i, i + 1) for i in range(count - 1)]
        backward = [(target, source) for source, target in forward]
        low = lax.ppermute(
            lax.slice_in_dim(block, block.shape[dim] - width, None, axis=dim), axis, forward
        )
        high = lax.ppermute(lax.slice_in_dim(block, 0, width, axis=dim), axis, backward)
        block = jnp.concatenate([low, block, high], axis=dim)
    return block


def laplace_local(padded, center):
    side = jnp.pad(center, ((0, 0), (0, 0), (1, 1), (1, 1)))
    total = padded[:, 2:] + padded[:, :-2]
    total = total + side[:, :, 2:, 1:-1] + side[:, :, :-2, 1:-1]
    total = total + side[:, :, 1:-1, 2:] + side[:, :, 1:-1, :-2]
    return total - 6.0 * center


def inject(values, local_cells, field_shape):
    flat = jnp.zeros(
        (field_shape[0], field_shape[1] * field_shape[2] * field_shape[3]), jnp.float32
    )
    return flat.at[:, local_cells].add(values).reshape(field_shape)


def inner_rows(rows):
    return lax.dot_general(
        rows,
        rows,
        (((1,), (1,)), ((), ())),
        precision=lax.Precision.HIGHEST,
        preferred_element_type=jnp.float32,
    )


def shards(
    courant_field,
    probe_fields,
    prior_weight,
    source_cells,
    source_strength,
    wavelet,
    receiver_cells,
    receiver_weight,
):
    field_shape = probe_fields.shape
    groups = field_shape[0]
    cells = field_shape[1] * field_shape[2] * field_shape[3]
    steps_total = wavelet.shape[0]
    offset = lax.axis_index("space") * cells
    source_local = source_cells - offset
    receiver_local = receiver_cells - offset
    source_field = (
        jnp.zeros((cells,), jnp.float32)
        .at[source_local]
        .add(source_strength)
        .reshape(field_shape[1:])
    )
    state_prev = jnp.zeros((groups + 1,) + field_shape[1:], jnp.float32)
    state_now = jnp.concatenate(
        [(wavelet[0] * source_field)[None], jnp.zeros(field_shape, jnp.float32)], 0
    )
    drives = [None]
    records = [None]
    for step in range(1, steps_total):
        padded = extended(state_now, (("space", 1),), 1)
        bent = laplace_local(padded, state_now)
        drive = courant_field * bent[0]
        forcing = jnp.concatenate(
            [(wavelet[step] * source_field)[None], probe_fields * drive[None]], 0
        )
        state_next = 2.0 * state_now - state_prev + courant_field * bent + forcing
        drives.append(drive)
        records.append(jnp.take(state_next[1:].reshape(groups, cells), receiver_local, axis=1))
        state_prev, state_now = (state_now, state_next)
    adjoint_next = inject(receiver_weight * records[steps_total - 1], receiver_local, field_shape)
    adjoint_after = jnp.zeros(field_shape, jnp.float32)
    hessian = prior_weight * probe_fields + drives[steps_total - 1] * adjoint_next
    for level in range(steps_total - 1, 1, -1):
        scaled = courant_field * adjoint_next
        padded = extended(scaled, (("space", 1),), 1)
        injected = inject(receiver_weight * records[level - 1], receiver_local, field_shape)
        adjoint_now = 2.0 * adjoint_next - adjoint_after + laplace_local(padded, scaled) + injected
        hessian = hessian + drives[level - 1] * adjoint_now
        adjoint_after, adjoint_next = (adjoint_next, adjoint_now)
    flat = hessian.reshape(groups, cells)
    total_cells = cells * lax.axis_size("space")
    rows = lax.all_gather(flat, "probe", axis=0, tiled=True)
    gram = lax.psum(inner_rows(rows), "space") / total_cells
    lower = jnp.linalg.cholesky(gram)
    solved = lax.linalg.triangular_solve(lower, rows, left_side=True, lower=True)
    mine = lax.dynamic_slice_in_dim(solved, lax.axis_index("probe") * groups, groups, 0)
    return (hessian, mine.reshape(field_shape))


def solution(mesh):
    in_specs = (
        P("space", None, None),
        P("probe", "space", None, None),
        P("space", None, None),
        P("space"),
        P("space"),
        P(),
        P("space"),
        P("space"),
    )
    out_specs = (P("probe", "space", None, None), P("probe", "space", None, None))
    return jax.shard_map(shards, mesh=mesh, in_specs=in_specs, out_specs=out_specs, check_vma=False)
```

profile of v0, /device:TPU:4, one launch (start us, length us, event | category | flops | bytes accessed | tf_op | source)
XLA Modules:
  0.0 436.4 jit_solution(6910389396807057819)
XLA Ops:
  7.2 1.6 fusion.184
  10.6 5.0 %broadcast_multiply_fusion.13 = (f32[16384]{0:T(1024)S(1)}, f32[16384]{0:T(1024)S(1)}, f32[16384]{0:T(1024)S(1)}, f32[16384]{0:T(1024)S(1)}, f32[16384]{0:T(1024...) fusion(f32[16384]{0:T(1024)S(1)} %scatter_custom_fusion, f32[]{:T(128)} %bitcast.14, f32[]{:T(128)} %bitcast.11, ...), kind=kLoop, calls=%fused_computation.264 | loop fusion | flops 131072 | bytes 589856 | tf_op jit(solution)/shard_map/mul | solution.py:79
  15.7 1.7 collective-permute-start.1
  17.4 1.3 collective-permute-start
  18.8 3.6 collective-permute-done
  25.6 5.8 %collective-permute-start.3 = (f32[5,1,32,256]{3,2,1,0:T(8,128)S(1)}, f32[5,1,32,256]{3,2,1,0:T(8,128)S(1)}, u32[]{:S(2)}, u32[]{:S(2)}) collective-permute-start(f32[5,1,32,256]{3,2,1,0:T(8,128)S(1)} %get-tuple-element.29), channel_id=1, source_target_pairs={{0,1},{1,2},{2,3},{3,4},{4,5},{5,6},{6,7},{7,8},{8,9},{9,10},{10,1... | collective-permute-start | bytes 491528 | tf_op jit(solution)/shard_map/ppermute | solution.py:12
  31.4 1.3 collective-permute-start.2
  32.7 2.0 collective-permute-done.2
  37.9 5.6 %collective-permute-start.5 = (f32[5,1,32,256]{3,2,1,0:T(8,128)S(1)}, f32[5,1,32,256]{3,2,1,0:T(8,128)S(1)}, u32[]{:S(2)}, u32[]{:S(2)}) collective-permute-start(f32[5,1,32,256]{3,2,1,0:T(8,128)S(1)} %get-tuple-element.27), channel_id=1, source_target_pairs={{0,1},{1,2},{2,3},{3,4},{4,5},{5,6},{6,7},{7,8},{8,9},{9,10},{10,1... | collective-permute-start | bytes 491528 | tf_op jit(solution)/shard_map/ppermute | solution.py:12
  43.4 1.3 collective-permute-start.4
  44.8 1.9 collective-permute-done.4
  47.4 5.6 %collective-permute-start.7 = (f32[5,1,32,256]{3,2,1,0:T(8,128)S(1)}, f32[5,1,32,256]{3,2,1,0:T(8,128)S(1)}, u32[]{:S(2)}, u32[]{:S(2)}) collective-permute-start(f32[5,1,32,256]{3,2,1,0:T(8,128)S(1)} %get-tuple-element.25), channel_id=1, source_target_pairs={{0,1},{1,2},{2,3},{3,4},{4,5},{5,6},{6,7},{7,8},{8,9},{9,10},{10,1... | collective-permute-start | bytes 491528 | tf_op jit(solution)/shard_map/ppermute | solution.py:12
  52.9 1.3 collective-permute-start.6
  54.3 2.0 collective-permute-done.6
  56.8 8.0 %collective-permute-start.9 = (f32[5,1,32,256]{3,2,1,0:T(8,128)S(1)}, f32[5,1,32,256]{3,2,1,0:T(8,128)S(1)}, u32[]{:S(2)}, u32[]{:S(2)}) collective-permute-start(f32[5,1,32,256]{3,2,1,0:T(8,128)S(1)} %get-tuple-element.23), channel_id=1, source_target_pairs={{0,1},{1,2},{2,3},{3,4},{4,5},{5,6},{6,7},{7,8},{8,9},{9,10},{10,1... | collective-permute-start | bytes 491528 | tf_op jit(solution)/shard_map/ppermute | solution.py:12
  64.8 1.3 collective-permute-start.8
  66.2 2.0 collective-permute-done.8
  68.7 6.5 %collective-permute-start.11 = (f32[5,1,32,256]{3,2,1,0:T(8,128)S(1)}, f32[5,1,32,256]{3,2,1,0:T(8,128)S(1)}, u32[]{:S(2)}, u32[]{:S(2)}) collective-permute-start(f32[5,1,32,256]{3,2,1,0:T(8,128)S(1)} %get-tuple-element.21), channel_id=1, source_target_pairs={{0,1},{1,2},{2,3},{3,4},{4,5},{5,6},{6,7},{7,8},{8,9},{9,10},{10,1... | collective-permute-start | bytes 491528 | tf_op jit(solution)/shard_map/ppermute | solution.py:12
  75.2 1.3 collective-permute-start.10
  76.6 1.9 collective-permute-done.10
  79.7 6.5 %collective-permute-start.13 = (f32[5,1,32,256]{3,2,1,0:T(8,128)S(1)}, f32[5,1,32,256]{3,2,1,0:T(8,128)S(1)}, u32[]{:S(2)}, u32[]{:S(2)}) collective-permute-start(f32[5,1,32,256]{3,2,1,0:T(8,128)S(1)} %get-tuple-element.19), channel_id=1, source_target_pairs={{0,1},{1,2},{2,3},{3,4},{4,5},{5,6},{6,7},{7,8},{8,9},{9,10},{10,1... | collective-permute-start | bytes 491528 | tf_op jit(solution)/shard_map/ppermute | solution.py:12
  86.2 1.3 collective-permute-start.12
  87.6 1.9 collective-permute-done.12
  89.9 4.7 %copy.29 = f32[4,2,32,256]{0,3,2,1:T(8,128)} copy(f32[4,2,32,256]{3,2,1,0:T(8,128)S(1)} %get-tuple-element.15) | data formatting | bytes 524288 | tf_op jit(solution)/shard_map/slice | solution.py:83
  94.6 5.5 %scatter_custom_fusion.1 = f32[4,16384]{0,1:T(8,128)} fusion(s32[64]{0:T(128)S(1)} %get-tuple-element.14, f32[]{:T(128)} %constant.69.clone.1, f32[]{:T(128)} %constant.78.clone.1, f32[64]{0:T(128)S(1)} %copy-done.10, pred[64]{0:T(512)(128)(4,1)S(1)} %get-tuple-element.13, f32[4,16384]{0,1:T(8,128)} %bitcast.125, s32[1024]{0:T(1024)S(1)} %pad_clamp_fusion), kind=kCustom, calls=%fused_computation.27 | custom fusion | flops 768 | bytes 529416 | tf_op jit(solution)/shard_map/scatter-add | solution.py:32
  100.2 5.2 %copy.30 = f32[4,2,32,256]{3,2,1,0:T(8,128)S(1)} copy(f32[4,2,32,256]{0,3,2,1:T(8,128)} %bitcast.126) | data formatting | bytes 524288 | tf_op jit(solution)/shard_map/reshape | solution.py:32
  106.1 6.5 %collective-permute-start.15 = (f32[4,1,32,256]{3,2,1,0:T(8,128)}, f32[4,1,32,256]{3,2,1,0:T(8,128)S(1)}, u32[]{:S(2)}, u32[]{:S(2)}) collective-permute-start(f32[4,1,32,256]{3,2,1,0:T(8,128)} %get-tuple-element.41), channel_id=1, source_target_pairs={{0,1},{1,2},{2,3},{3,4},{4,5},{5,6},{6,7},{7,8},{8,9},{9,10},{10,1... | collective-permute-start | bytes 393224 | tf_op jit(solution)/shard_map/ppermute | solution.py:12
  112.6 1.3 collective-permute-start.14
  113.9 4.7 %copy.33 = f32[4,2,32,256]{0,3,2,1:T(8,128)} copy(f32[4,2,32,256]{3,2,1,0:T(8,128)S(1)} %get-tuple-element.16) | data formatting | bytes 524288 | tf_op jit(solution)/shard_map/slice | solution.py:83
  118.6 5.5 %scatter_custom_fusion.2 = f32[4,16384]{0,1:T(8,128)} fusion(s32[64]{0:T(128)S(1)} %get-tuple-element.14, f32[]{:T(128)} %constant.69.clone.1, f32[]{:T(128)} %constant.78.clone.1, f32[64]{0:T(128)S(1)} %copy-done.10, pred[64]{0:T(512)(128)(4,1)S(1)} %get-tuple-element.13, f32[4,16384]{0,1:T(8,128)} %bitcast.127, s32[1024]{0:T(1024)S(1)} %pad_clamp_fusion), kind=kCustom, calls=%fused_computation.25 | custom fusion | flops 768 | bytes 529416 | tf_op jit(solution)/shard_map/scatter-add | solution.py:32
  124.2 5.2 %copy.34 = f32[4,2,32,256]{3,2,1,0:T(8,128)S(1)} copy(f32[4,2,32,256]{0,3,2,1:T(8,128)} %bitcast.128) | data formatting | bytes 524288 | tf_op jit(solution)/shard_map/reshape | solution.py:32
  131.3 3.7 collective-permute-start.17
  135.0 1.5 collective-permute-start.16
  136.5 4.7 %copy.36 = f32[4,2,32,256]{0,3,2,1:T(8,128)} copy(f32[4,2,32,256]{3,2,1,0:T(8,128)S(1)} %get-tuple-element.17) | data formatting | bytes 524288 | tf_op jit(solution)/shard_map/slice | solution.py:83
  141.2 5.5 %scatter_custom_fusion.3 = f32[4,16384]{0,1:T(8,128)} fusion(s32[64]{0:T(128)S(1)} %get-tuple-element.14, f32[]{:T(128)} %constant.69.clone.1, f32[]{:T(128)} %constant.78.clone.1, f32[64]{0:T(128)S(1)} %copy-done.10, pred[64]{0:T(512)(128)(4,1)S(1)} %get-tuple-element.13, f32[4,16384]{0,1:T(8,128)} %bitcast.129, s32[1024]{0:T(1024)S(1)} %pad_clamp_fusion), kind=kCustom, calls=%fused_computation.23 | custom fusion | flops 768 | bytes 529416 | tf_op jit(solution)/shard_map/scatter-add | solution.py:32
  146.7 5.2 %copy.37 = f32[4,2,32,256]{3,2,1,0:T(8,128)S(1)} copy(f32[4,2,32,256]{0,3,2,1:T(8,128)} %bitcast.130) | data formatting | bytes 524288 | tf_op jit(solution)/shard_map/reshape | solution.py:32
  153.9 5.0 %collective-permute-start.19 = (f32[4,1,32,256]{3,2,1,0:T(8,128)}, f32[4,1,32,256]{3,2,1,0:T(8,128)}, u32[]{:S(2)}, u32[]{:S(2)}) collective-permute-start(f32[4,1,32,256]{3,2,1,0:T(8,128)} %get-tuple-element.37), channel_id=1, source_target_pairs={{0,1},{1,2},{2,3},{3,4},{4,5},{5,6},{6,7},{7,8},{8,9},{9,10},{10,1... | collective-permute-start | bytes 393224 | tf_op jit(solution)/shard_map/ppermute | solution.py:12
  158.9 1.3 collective-permute-start.18
  160.2 4.7 %copy.38 = f32[4,2,32,256]{0,3,2,1:T(8,128)} copy(f32[4,2,32,256]{3,2,1,0:T(8,128)S(1)} %slice.584) | data formatting | bytes 524288 | tf_op jit(solution)/shard_map/slice | solution.py:83
  164.9 5.5 %scatter_custom_fusion.4 = f32[4,16384]{0,1:T(8,128)} fusion(s32[64]{0:T(128)S(1)} %get-tuple-element.14, f32[]{:T(128)} %constant.69.clone.1, f32[]{:T(128)} %constant.78.clone.1, f32[64]{0:T(128)S(1)} %copy-done.10, pred[64]{0:T(512)(128)(4,1)S(1)} %get-tuple-element.13, f32[4,16384]{0,1:T(8,128)} %bitcast.131, s32[1024]{0:T(1024)S(1)} %pad_clamp_fusion), kind=kCustom, calls=%fused_computation.21 | custom fusion | flops 768 | bytes 529416 | tf_op jit(solution)/shard_map/scatter-add | solution.py:32
  170.5 5.2 %copy.39 = f32[4,2,32,256]{3,2,1,0:T(8,128)S(1)} copy(f32[4,2,32,256]{0,3,2,1:T(8,128)} %bitcast.132) | data formatting | bytes 524288 | tf_op jit(solution)/shard_map/reshape | solution.py:32
  175.7 1.2 broadcast_multiply_fusion.2
  177.7 4.3 collective-permute-start.21
  181.9 1.3 collective-permute-start.20
  183.2 4.7 %copy.40 = f32[4,2,32,256]{0,3,2,1:T(8,128)} copy(f32[4,2,32,256]{3,2,1,0:T(8,128)S(1)} %slice.587) | data formatting | bytes 524288 | tf_op jit(solution)/shard_map/slice | solution.py:83
  188.0 5.5 %scatter_custom_fusion.5 = f32[4,16384]{0,1:T(8,128)} fusion(s32[64]{0:T(128)S(1)} %get-tuple-element.14, f32[]{:T(128)} %constant.69.clone.1, f32[]{:T(128)} %constant.78.clone.1, f32[64]{0:T(128)S(1)} %copy-done.10, pred[64]{0:T(512)(128)(4,1)S(1)} %get-tuple-element.13, f32[4,16384]{0,1:T(8,128)} %bitcast.133, s32[1024]{0:T(1024)S(1)} %pad_clamp_fusion), kind=kCustom, calls=%fused_computation.19 | custom fusion | flops 768 | bytes 529416 | tf_op jit(solution)/shard_map/scatter-add | solution.py:32
  193.5 5.2 %copy.41 = f32[4,2,32,256]{3,2,1,0:T(8,128)S(1)} copy(f32[4,2,32,256]{0,3,2,1:T(8,128)} %bitcast.134) | data formatting | bytes 524288 | tf_op jit(solution)/shard_map/reshape | solution.py:32
  200.0 4.3 collective-permute-start.23
  204.3 1.3 collective-permute-start.22
  205.6 4.7 %copy.42 = f32[4,2,32,256]{0,3,2,1:T(8,128)} copy(f32[4,2,32,256]{3,2,1,0:T(8,128)S(1)} %slice.590) | data formatting | bytes 524288 | tf_op jit(solution)/shard_map/slice | solution.py:83
  210.3 5.5 %scatter_custom_fusion.6 = f32[4,16384]{0,1:T(8,128)} fusion(s32[64]{0:T(128)S(1)} %get-tuple-element.14, f32[]{:T(128)} %constant.69.clone.1, f32[]{:T(128)} %constant.78.clone.1, f32[64]{0:T(128)S(1)} %copy-done.10, pred[64]{0:T(512)(128)(4,1)S(1)} %get-tuple-element.13, f32[4,16384]{0,1:T(8,128)} %bitcast.135, s32[1024]{0:T(1024)S(1)} %pad_clamp_fusion), kind=kCustom, calls=%fused_computation.17 | custom fusion | flops 768 | bytes 529416 | tf_op jit(solution)/shard_map/scatter-add | solution.py:32
  215.9 5.2 %copy.43 = f32[4,2,32,256]{3,2,1,0:T(8,128)S(1)} copy(f32[4,2,32,256]{0,3,2,1:T(8,128)} %bitcast.136) | data formatting | bytes 524288 | tf_op jit(solution)/shard_map/reshape | solution.py:32
  222.3 3.6 collective-permute-start.25
  226.0 1.5 collective-permute-start.24
  227.5 4.7 %copy.44 = f32[4,2,32,256]{0,3,2,1:T(8,128)} copy(f32[4,2,32,256]{3,2,1,0:T(8,128)S(1)} %slice.593) | data formatting | bytes 524288 | tf_op jit(solution)/shard_map/slice | solution.py:83
  232.3 5.5 %scatter_custom_fusion.7 = f32[4,16384]{0,1:T(8,128)} fusion(s32[64]{0:T(128)S(1)} %get-tuple-element.14, f32[]{:T(128)} %constant.69.clone.1, f32[]{:T(128)} %constant.78.clone.1, f32[64]{0:T(128)S(1)} %copy-done.10, pred[64]{0:T(512)(128)(4,1)S(1)} %get-tuple-element.13, f32[4,16384]{0,1:T(8,128)} %bitcast.123, s32[1024]{0:T(1024)S(1)} %pad_clamp_fusion), kind=kCustom, calls=%fused_computation.15 | custom fusion | flops 768 | bytes 529416 | tf_op jit(solution)/shard_map/scatter-add | solution.py:32
  237.8 5.3 %copy.45 = f32[4,2,32,256]{3,2,1,0:T(8,128)S(1)} copy(f32[4,2,32,256]{0,3,2,1:T(8,128)} %bitcast.124) | data formatting | bytes 524288 | tf_op jit(solution)/shard_map/reshape | solution.py:32
  243.8 1.4 fusion.103
  246.0 45.0 %all-gather.3.cloned.1.call-done = f32[4,4,16384]{2,1,0:T(4,128)} async-done(((f32[1,4,16384]{2,1,0:T(4,128)}), f32[4,4,16384]{2,1,0:T(4,128)}) %all-gather.3.cloned.1.call-update) | async-done | bytes 1048592 | tf_op jit(solution)/shard_map/all_gather | solution.py:97
  291.0 1.6 reshape.325
  292.6 1.5 fusion.185
  294.1 129.5 %psum.7 = f32[16,16]{0,1:T(8,128)S(1)} all-reduce(f32[16,16]{0,1:T(8,128)S(1)} %fusion.185), channel_id=1, replica_groups=mesh['probe'=4,'space'=64] {'space'}, use_global_device_ids=true, to_apply=%region_8.10 | all-reduce | flops 256 | bytes 2048 | tf_op jit(solution)/shard_map/psum | solution.py:98
  423.7 1.5 cholesky.16
  426.5 1.2 custom-call.6
  (118 shorter events, 24.2 us)
Async XLA Ops:
  7.2 39.8 %copy-start = (f32[2,32,256]{2,1,0:T(8,128)S(1)}, f32[2,32,256]{2,1,0:T(8,128)}, u32[]{:S(2)}) copy-start(f32[2,32,256]{2,1,0:T(8,128)} %param.10) | copy-start | bytes 196612
  7.2 39.8 %copy-start.1 = (f32[4,2,32,256]{3,2,1,0:T(8,128)S(1)}, f32[4,2,32,256]{3,2,1,0:T(8,128)}, u32[]{:S(2)}) copy-start(f32[4,2,32,256]{3,2,1,0:T(8,128)} %param.11) | copy-start | bytes 786436
  7.2 283.8 %all-gather.3.cloned.1.call-start = ((), (), s32[]{:S(2)}) async-start(), calls=%async_computation | async-start | bytes 1310720 | tf_op jit(solution)/shard_map/all_gather | solution.py:97
  15.7 3.1 collective-permute-start.1
  17.4 5.0 %collective-permute-start = (f32[5,1,32,256]{3,2,1,0:T(8,128)S(1)}, f32[5,1,32,256]{3,2,1,0:T(8,128)S(1)}, u32[]{:S(2)}, u32[]{:S(2)}) collective-permute-start(f32[5,1,32,256]{3,2,1,0:T(8,128)S(1)} %get-tuple-element.50), channel_id=1, source_target_pairs={{1,0},{2,1},{3,2},{4,3},{5,4},{6,5},{7,6},{8,7},{9,8},{10,9},{11,1... | collective-permute-start | bytes 491528 | tf_op jit(solution)/shard_map/ppermute | solution.py:15
  25.6 7.1 %collective-permute-start.3 = (f32[5,1,32,256]{3,2,1,0:T(8,128)S(1)}, f32[5,1,32,256]{3,2,1,0:T(8,128)S(1)}, u32[]{:S(2)}, u32[]{:S(2)}) collective-permute-start(f32[5,1,32,256]{3,2,1,0:T(8,128)S(1)} %get-tuple-element.29), channel_id=1, source_target_pairs={{0,1},{1,2},{2,3},{3,4},{4,5},{5,6},{6,7},{7,8},{8,9},{9,10},{10,1... | collective-permute-start | bytes 491528 | tf_op jit(solution)/shard_map/ppermute | solution.py:12
  31.4 3.3 collective-permute-start.2
  37.9 6.9 %collective-permute-start.5 = (f32[5,1,32,256]{3,2,1,0:T(8,128)S(1)}, f32[5,1,32,256]{3,2,1,0:T(8,128)S(1)}, u32[]{:S(2)}, u32[]{:S(2)}) collective-permute-start(f32[5,1,32,256]{3,2,1,0:T(8,128)S(1)} %get-tuple-element.27), channel_id=1, source_target_pairs={{0,1},{1,2},{2,3},{3,4},{4,5},{5,6},{6,7},{7,8},{8,9},{9,10},{10,1... | collective-permute-start | bytes 491528 | tf_op jit(solution)/shard_map/ppermute | solution.py:12
  43.4 3.3 collective-permute-start.4
  44.8 42.8 %copy-start.11 = (s32[64]{0:T(128)S(1)}, s32[64]{0:T(128)}, u32[]{:S(2)}) copy-start(s32[64]{0:T(128)} %param.16) | copy-start | bytes 772
  47.4 6.9 %collective-permute-start.7 = (f32[5,1,32,256]{3,2,1,0:T(8,128)S(1)}, f32[5,1,32,256]{3,2,1,0:T(8,128)S(1)}, u32[]{:S(2)}, u32[]{:S(2)}) collective-permute-start(f32[5,1,32,256]{3,2,1,0:T(8,128)S(1)} %get-tuple-element.25), channel_id=1, source_target_pairs={{0,1},{1,2},{2,3},{3,4},{4,5},{5,6},{6,7},{7,8},{8,9},{9,10},{10,1... | collective-permute-start | bytes 491528 | tf_op jit(solution)/shard_map/ppermute | solution.py:12
  52.9 3.3 collective-permute-start.6
  56.8 9.3 %collective-permute-start.9 = (f32[5,1,32,256]{3,2,1,0:T(8,128)S(1)}, f32[5,1,32,256]{3,2,1,0:T(8,128)S(1)}, u32[]{:S(2)}, u32[]{:S(2)}) collective-permute-start(f32[5,1,32,256]{3,2,1,0:T(8,128)S(1)} %get-tuple-element.23), channel_id=1, source_target_pairs={{0,1},{1,2},{2,3},{3,4},{4,5},{5,6},{6,7},{7,8},{8,9},{9,10},{10,1... | collective-permute-start | bytes 491528 | tf_op jit(solution)/shard_map/ppermute | solution.py:12
  64.8 3.3 collective-permute-start.8
  68.7 7.8 %collective-permute-start.11 = (f32[5,1,32,256]{3,2,1,0:T(8,128)S(1)}, f32[5,1,32,256]{3,2,1,0:T(8,128)S(1)}, u32[]{:S(2)}, u32[]{:S(2)}) collective-permute-start(f32[5,1,32,256]{3,2,1,0:T(8,128)S(1)} %get-tuple-element.21), channel_id=1, source_target_pairs={{0,1},{1,2},{2,3},{3,4},{4,5},{5,6},{6,7},{7,8},{8,9},{9,10},{10,1... | collective-permute-start | bytes 491528 | tf_op jit(solution)/shard_map/ppermute | solution.py:12
  75.2 3.3 collective-permute-start.10
  76.5 18.1 %copy-start.10 = (f32[64]{0:T(128)S(1)}, f32[64]{0:T(128)}, u32[]{:S(2)}) copy-start(f32[64]{0:T(128)} %param.17) | copy-start | bytes 772
  78.8 0.6 copy-start.3
  79.7 7.9 %collective-permute-start.13 = (f32[5,1,32,256]{3,2,1,0:T(8,128)S(1)}, f32[5,1,32,256]{3,2,1,0:T(8,128)S(1)}, u32[]{:S(2)}, u32[]{:S(2)}) collective-permute-start(f32[5,1,32,256]{3,2,1,0:T(8,128)S(1)} %get-tuple-element.19), channel_id=1, source_target_pairs={{0,1},{1,2},{2,3},{3,4},{4,5},{5,6},{6,7},{7,8},{8,9},{9,10},{10,1... | collective-permute-start | bytes 491528 | tf_op jit(solution)/shard_map/ppermute | solution.py:12
  86.2 3.3 collective-permute-start.12
  89.8 10.4 %copy-start.5 = (f32[2,32,256]{2,1,0:T(8,128)}, f32[2,32,256]{2,1,0:T(8,128)S(1)}, u32[]{:S(2)}) copy-start(f32[2,32,256]{2,1,0:T(8,128)S(1)} %fusion.112) | copy-start | bytes 196612
  106.1 23.3 %collective-permute-start.15 = (f32[4,1,32,256]{3,2,1,0:T(8,128)}, f32[4,1,32,256]{3,2,1,0:T(8,128)S(1)}, u32[]{:S(2)}, u32[]{:S(2)}) collective-permute-start(f32[4,1,32,256]{3,2,1,0:T(8,128)} %get-tuple-element.41), channel_id=1, source_target_pairs={{0,1},{1,2},{2,3},{3,4},{4,5},{5,6},{6,7},{7,8},{8,9},{9,10},{10,1... | collective-permute-start | bytes 393224 | tf_op jit(solution)/shard_map/ppermute | solution.py:12
  112.6 17.5 %collective-permute-start.14 = (f32[4,1,32,256]{3,2,1,0:T(8,128)S(1)}, f32[4,1,32,256]{3,2,1,0:T(8,128)}, u32[]{:S(2)}, u32[]{:S(2)}) collective-permute-start(f32[4,1,32,256]{3,2,1,0:T(8,128)S(1)} %get-tuple-element.40), channel_id=1, source_target_pairs={{1,0},{2,1},{3,2},{4,3},{5,4},{6,5},{7,6},{8,7},{9,8},{10,9},{11,1... | collective-permute-start | bytes 393224 | tf_op jit(solution)/shard_map/ppermute | solution.py:15
  129.4 0.7 copy-start.7
  131.3 20.7 %collective-permute-start.17 = (f32[4,1,32,256]{3,2,1,0:T(8,128)S(1)}, f32[4,1,32,256]{3,2,1,0:T(8,128)}, u32[]{:S(2)}, u32[]{:S(2)}) collective-permute-start(f32[4,1,32,256]{3,2,1,0:T(8,128)S(1)} %get-tuple-element.39), channel_id=1, source_target_pairs={{0,1},{1,2},{2,3},{3,4},{4,5},{5,6},{6,7},{7,8},{8,9},{9,10},{10,1... | collective-permute-start | bytes 393224 | tf_op jit(solution)/shard_map/ppermute | solution.py:12
  135.0 17.0 %collective-permute-start.16 = (f32[4,1,32,256]{3,2,1,0:T(8,128)S(1)}, f32[4,1,32,256]{3,2,1,0:T(8,128)}, u32[]{:S(2)}, u32[]{:S(2)}) collective-permute-start(f32[4,1,32,256]{3,2,1,0:T(8,128)S(1)} %get-tuple-element.38), channel_id=1, source_target_pairs={{1,0},{2,1},{3,2},{4,3},{5,4},{6,5},{7,6},{8,7},{9,8},{10,9},{11,1... | collective-permute-start | bytes 393224 | tf_op jit(solution)/shard_map/ppermute | solution.py:15
  153.9 21.8 %collective-permute-start.19 = (f32[4,1,32,256]{3,2,1,0:T(8,128)}, f32[4,1,32,256]{3,2,1,0:T(8,128)}, u32[]{:S(2)}, u32[]{:S(2)}) collective-permute-start(f32[4,1,32,256]{3,2,1,0:T(8,128)} %get-tuple-element.37), channel_id=1, source_target_pairs={{0,1},{1,2},{2,3},{3,4},{4,5},{5,6},{6,7},{7,8},{8,9},{9,10},{10,1... | collective-permute-start | bytes 393224 | tf_op jit(solution)/shard_map/ppermute | solution.py:12
  158.9 16.8 %collective-permute-start.18 = (f32[4,1,32,256]{3,2,1,0:T(8,128)}, f32[4,1,32,256]{3,2,1,0:T(8,128)}, u32[]{:S(2)}, u32[]{:S(2)}) collective-permute-start(f32[4,1,32,256]{3,2,1,0:T(8,128)} %get-tuple-element.36), channel_id=1, source_target_pairs={{1,0},{2,1},{3,2},{4,3},{5,4},{6,5},{7,6},{8,7},{9,8},{10,9},{11,1... | collective-permute-start | bytes 393224 | tf_op jit(solution)/shard_map/ppermute | solution.py:15
  177.7 21.1 %collective-permute-start.21 = (f32[4,1,32,256]{3,2,1,0:T(8,128)}, f32[4,1,32,256]{3,2,1,0:T(8,128)}, u32[]{:S(2)}, u32[]{:S(2)}) collective-permute-start(f32[4,1,32,256]{3,2,1,0:T(8,128)} %get-tuple-element.35), channel_id=1, source_target_pairs={{0,1},{1,2},{2,3},{3,4},{4,5},{5,6},{6,7},{7,8},{8,9},{9,10},{10,1... | collective-permute-start | bytes 393224 | tf_op jit(solution)/shard_map/ppermute | solution.py:12
  181.9 16.8 %collective-permute-start.20 = (f32[4,1,32,256]{3,2,1,0:T(8,128)}, f32[4,1,32,256]{3,2,1,0:T(8,128)}, u32[]{:S(2)}, u32[]{:S(2)}) collective-permute-start(f32[4,1,32,256]{3,2,1,0:T(8,128)} %get-tuple-element.34), channel_id=1, source_target_pairs={{1,0},{2,1},{3,2},{4,3},{5,4},{6,5},{7,6},{8,7},{9,8},{10,9},{11,1... | collective-permute-start | bytes 393224 | tf_op jit(solution)/shard_map/ppermute | solution.py:15
  200.0 21.1 %collective-permute-start.23 = (f32[4,1,32,256]{3,2,1,0:T(8,128)S(1)}, f32[4,1,32,256]{3,2,1,0:T(8,128)}, u32[]{:S(2)}, u32[]{:S(2)}) collective-permute-start(f32[4,1,32,256]{3,2,1,0:T(8,128)S(1)} %get-tuple-element.33), channel_id=1, source_target_pairs={{0,1},{1,2},{2,3},{3,4},{4,5},{5,6},{6,7},{7,8},{8,9},{9,10},{10,1... | collective-permute-start | bytes 393224 | tf_op jit(solution)/shard_map/ppermute | solution.py:12
  204.3 16.8 %collective-permute-start.22 = (f32[4,1,32,256]{3,2,1,0:T(8,128)S(1)}, f32[4,1,32,256]{3,2,1,0:T(8,128)}, u32[]{:S(2)}, u32[]{:S(2)}) collective-permute-start(f32[4,1,32,256]{3,2,1,0:T(8,128)S(1)} %get-tuple-element.32), channel_id=1, source_target_pairs={{1,0},{2,1},{3,2},{4,3},{5,4},{6,5},{7,6},{8,7},{9,8},{10,9},{11,1... | collective-permute-start | bytes 393224 | tf_op jit(solution)/shard_map/ppermute | solution.py:15
  222.3 20.7 %collective-permute-start.25 = (f32[4,1,32,256]{3,2,1,0:T(8,128)S(1)}, f32[4,1,32,256]{3,2,1,0:T(8,128)S(1)}, u32[]{:S(2)}, u32[]{:S(2)}) collective-permute-start(f32[4,1,32,256]{3,2,1,0:T(8,128)S(1)} %get-tuple-element.31), channel_id=1, source_target_pairs={{0,1},{1,2},{2,3},{3,4},{4,5},{5,6},{6,7},{7,8},{8,9},{9,10},{10,1... | collective-permute-start | bytes 393224 | tf_op jit(solution)/shard_map/ppermute | solution.py:12
  226.0 17.1 %collective-permute-start.24 = (f32[4,1,32,256]{3,2,1,0:T(8,128)S(1)}, f32[4,1,32,256]{3,2,1,0:T(8,128)}, u32[]{:S(2)}, u32[]{:S(2)}) collective-permute-start(f32[4,1,32,256]{3,2,1,0:T(8,128)S(1)} %get-tuple-element.30), channel_id=1, source_target_pairs={{1,0},{2,1},{3,2},{4,3},{5,4},{6,5},{7,6},{8,7},{9,8},{10,9},{11,1... | collective-permute-start | bytes 393224 | tf_op jit(solution)/shard_map/ppermute | solution.py:15
  237.8 6.0 %copy-start.4 = (f32[2,32,256]{2,1,0:T(8,128)S(1)}, f32[2,32,256]{2,1,0:T(8,128)}, u32[]{:S(2)}) copy-start(f32[2,32,256]{2,1,0:T(8,128)} %copy-done.3) | copy-start | bytes 196612
  237.8 6.0 %copy-start.6 = (f32[2,32,256]{2,1,0:T(8,128)S(1)}, f32[2,32,256]{2,1,0:T(8,128)}, u32[]{:S(2)}) copy-start(f32[2,32,256]{2,1,0:T(8,128)} %copy-done.5) | copy-start | bytes 196612
  237.8 6.0 %copy-start.9 = (f32[2,32,256]{2,1,0:T(8,128)S(1)}, f32[2,32,256]{2,1,0:T(8,128)}, u32[]{:S(2)}) copy-start(f32[2,32,256]{2,1,0:T(8,128)} %param.12) | copy-start | bytes 196612
  243.1 0.7 copy-start.8
  245.1 184.5 %copy-start.2 = (f32[4,2,32,256]{3,2,1,0:T(8,128)}, f32[4,2,32,256]{3,2,1,0:T(8,128)S(1)}, u32[]{:S(2)}) copy-start(f32[4,2,32,256]{3,2,1,0:T(8,128)S(1)} %fusion.103) | copy-start | bytes 786436
Sparse Core Ops, SparseCore 0:
  246.1 44.8 all-gather.2
where the time goes:
time: 438 us; the launch traced here: 436 us
  blocking collectives  129 us (29%)
  starting transfers between devices  84.1 us (19%)
  local copies, waits for them, and re-layouts  79.3 us (18%)
  other arithmetic  65.7 us (15%)
  waiting for transfers between devices  60.3 us (14%)
  between operations  15 us (3%)
    psum x1, blocking collectives, shards(): gram = lax.psum(inner_rows(rows), 'space') / total_cells  129 us
    ppermute x13, starting transfers between devices, extended(): lax.ppermute(lax.slice_in_dim(block, block.shape[dim] - width, None, axis...  66.9 us
    all_gather x1, waiting for transfers between devices, shards(): rows = lax.all_gather(flat, 'probe', axis=0, tiled=True)  45 us
    scatter-add x7, other arithmetic, inject(): return flat.at[:, local_cells].add(values).reshape(field_shape)  38.7 us
    reshape x7, local copies, waits for them, and re-layouts, inject(): return flat.at[:, local_cells].add(values).reshape(field_shape)  36.7 us
    slice x11, local copies, waits for them, and re-layouts, shards(): state_next[1:].reshape(groups, cells)  33.2 us
    ppermute x13, starting transfers between devices, extended(): lax.ppermute(lax.slice_in_dim(block, 0, width, axis=dim), axis, backward)  17.1 us
    ppermute x13, waiting for transfers between devices, extended(): lax.ppermute(lax.slice_in_dim(block, 0, width, axis=dim), axis, backward)  15.3 us
  transfers between devices with their start and end apart: 27, of which 8 were waited for; matrix products, arithmetic and copies ran while one was open for 21% of the time, Pallas kernels for 0%

commit v1 on v0

--- a/solution.py
+++ b/solution.py
@@ -2,6 +2,12 @@
 import jax.numpy as jnp
 from jax import lax
 from jax.sharding import PartitionSpec as P
+
+
+def summed_here(block, axis):
+    parts = lax.all_gather(block, axis, axis=0, tiled=False)
+    acc = parts.sum(axis=0)
+    return acc
 
 
 def extended(block, sides, width):
@@ -95,7 +101,7 @@
     flat = hessian.reshape(groups, cells)
     total_cells = cells * lax.axis_size("space")
     rows = lax.all_gather(flat, "probe", axis=0, tiled=True)
-    gram = lax.psum(inner_rows(rows), "space") / total_cells
+    gram = summed_here(inner_rows(rows), "space") / total_cells
     lower = jnp.linalg.cholesky(gram)
     solved = lax.linalg.triangular_solve(lower, rows, left_side=True, lower=True)
     mine = lax.dynamic_slice_in_dim(solved, lax.axis_index("probe") * groups, groups, 0)

time: 438 us -> 360 us (0.82)
  blocking collectives: 129 us -> 51.3 us
    psum x1 -> x0, blocking collectives: 129 us -> none  [shards(): gram = lax.psum(inner_rows(rows), 'space') / total_cells]
    all_gather x0 -> x1, blocking collectives: none -> 51.3 us  [summed_here(): parts = lax.all_gather(block, axis, axis=0, tiled=False)]
  transfers between devices with their start and end apart: 27 -> 27, of which waited for: 8 -> 8; matrix products, arithmetic and copies ran while one was open for 21% -> 26% of each run, Pallas kernels for 0% -> 0%
where the time goes in v1:
time: 360 us; the launch traced here: 356 us
  starting transfers between devices  84.1 us (23%)
  local copies, waits for them, and re-layouts  79.8 us (22%)
  other arithmetic  63.1 us (18%)
  waiting for transfers between devices  60.4 us (17%)
  blocking collectives  51.3 us (14%)
  between operations  15.1 us (4%)
    ppermute x13, starting transfers between devices, extended(): lax.ppermute(lax.slice_in_dim(block, block.shape[dim] - width, None, axis...  66.9 us
    all_gather x1, blocking collectives, summed_here(): parts = lax.all_gather(block, axis, axis=0, tiled=False)  51.3 us
    all_gather x1, waiting for transfers between devices, shards(): rows = lax.all_gather(flat, 'probe', axis=0, tiled=True)  45.1 us
    scatter-add x7, other arithmetic, inject(): return flat.at[:, local_cells].add(values).reshape(field_shape)  39 us
    reshape x7, local copies, waits for them, and re-layouts, inject(): return flat.at[:, local_cells].add(values).reshape(field_shape)  36.7 us
    slice x11, local copies, waits for them, and re-layouts, shards(): state_next[1:].reshape(groups, cells)  33.2 us
    ppermute x13, starting transfers between devices, extended(): lax.ppermute(lax.slice_in_dim(block, 0, width, axis=dim), axis, backward)  17.2 us
    ppermute x13, waiting for transfers between devices, extended(): lax.ppermute(lax.slice_in_dim(block, 0, width, axis=dim), axis, backward)  15.3 us
  transfers between devices with their start and end apart: 27, of which 8 were waited for; matrix products, arithmetic and copies ran while one was open for 26% of the time, Pallas kernels for 0%

profile of v1, /device:TPU:4, one launch (start us, length us, event | category | flops | bytes accessed | tf_op | source)
XLA Modules:
  0.0 356.3 jit_solution(1140678241477410485)
XLA Ops:
  7.2 1.6 fusion.184
  10.6 5.0 %broadcast_multiply_fusion.13 = (f32[16384]{0:T(1024)S(1)}, f32[16384]{0:T(1024)S(1)}, f32[16384]{0:T(1024)S(1)}, f32[16384]{0:T(1024)S(1)}, f32[16384]{0:T(1024...) fusion(f32[16384]{0:T(1024)S(1)} %scatter_custom_fusion, f32[]{:T(128)} %bitcast.14, f32[]{:T(128)} %bitcast.11, ...), kind=kLoop, calls=%fused_computation.264 | loop fusion | flops 131072 | bytes 589856 | tf_op jit(solution)/shard_map/mul | solution.py:85
  15.6 1.7 collective-permute-start.1
  17.4 1.3 collective-permute-start
  18.7 3.6 %collective-permute-done = f32[5,1,32,256]{3,2,1,0:T(8,128)S(1)} collective-permute-done((f32[5,1,32,256]{3,2,1,0:T(8,128)S(1)}, f32[5,1,32,256]{3,2,1,0:T(8,128)S(1)}, u32[]{:S(2)}, u32[]{:S(2)}) %collective-permute-start) | collective-permute-done | bytes 163872 | tf_op jit(solution)/shard_map/ppermute | solution.py:21
  25.6 5.8 %collective-permute-start.3 = (f32[5,1,32,256]{3,2,1,0:T(8,128)S(1)}, f32[5,1,32,256]{3,2,1,0:T(8,128)S(1)}, u32[]{:S(2)}, u32[]{:S(2)}) collective-permute-start(f32[5,1,32,256]{3,2,1,0:T(8,128)S(1)} %get-tuple-element.29), channel_id=1, source_target_pairs={{0,1},{1,2},{2,3},{3,4},{4,5},{5,6},{6,7},{7,8},{8,9},{9,10},{10,1... | collective-permute-start | bytes 491528 | tf_op jit(solution)/shard_map/ppermute | solution.py:18
  31.3 1.3 collective-permute-start.2
  32.7 2.0 collective-permute-done.2
  38.5 5.6 %collective-permute-start.5 = (f32[5,1,32,256]{3,2,1,0:T(8,128)S(1)}, f32[5,1,32,256]{3,2,1,0:T(8,128)S(1)}, u32[]{:S(2)}, u32[]{:S(2)}) collective-permute-start(f32[5,1,32,256]{3,2,1,0:T(8,128)S(1)} %get-tuple-element.27), channel_id=1, source_target_pairs={{0,1},{1,2},{2,3},{3,4},{4,5},{5,6},{6,7},{7,8},{8,9},{9,10},{10,1... | collective-permute-start | bytes 491528 | tf_op jit(solution)/shard_map/ppermute | solution.py:18
  44.0 1.3 collective-permute-start.4
  45.4 1.9 collective-permute-done.4
  48.6 5.6 %collective-permute-start.7 = (f32[5,1,32,256]{3,2,1,0:T(8,128)S(1)}, f32[5,1,32,256]{3,2,1,0:T(8,128)S(1)}, u32[]{:S(2)}, u32[]{:S(2)}) collective-permute-start(f32[5,1,32,256]{3,2,1,0:T(8,128)S(1)} %get-tuple-element.25), channel_id=1, source_target_pairs={{0,1},{1,2},{2,3},{3,4},{4,5},{5,6},{6,7},{7,8},{8,9},{9,10},{10,1... | collective-permute-start | bytes 491528 | tf_op jit(solution)/shard_map/ppermute | solution.py:18
  54.1 1.3 collective-permute-start.6
  55.5 2.0 collective-permute-done.6
  58.6 8.0 %collective-permute-start.9 = (f32[5,1,32,256]{3,2,1,0:T(8,128)S(1)}, f32[5,1,32,256]{3,2,1,0:T(8,128)S(1)}, u32[]{:S(2)}, u32[]{:S(2)}) collective-permute-start(f32[5,1,32,256]{3,2,1,0:T(8,128)S(1)} %get-tuple-element.23), channel_id=1, source_target_pairs={{0,1},{1,2},{2,3},{3,4},{4,5},{5,6},{6,7},{7,8},{8,9},{9,10},{10,1... | collective-permute-start | bytes 491528 | tf_op jit(solution)/shard_map/ppermute | solution.py:18
  66.6 1.3 collective-permute-start.8
  68.0 2.0 collective-permute-done.8
  71.2 6.5 %collective-permute-start.11 = (f32[5,1,32,256]{3,2,1,0:T(8,128)S(1)}, f32[5,1,32,256]{3,2,1,0:T(8,128)S(1)}, u32[]{:S(2)}, u32[]{:S(2)}) collective-permute-start(f32[5,1,32,256]{3,2,1,0:T(8,128)S(1)} %get-tuple-element.21), channel_id=1, source_target_pairs={{0,1},{1,2},{2,3},{3,4},{4,5},{5,6},{6,7},{7,8},{8,9},{9,10},{10,1... | collective-permute-start | bytes 491528 | tf_op jit(solution)/shard_map/ppermute | solution.py:18
  77.6 1.3 collective-permute-start.10
  79.0 1.9 collective-permute-done.10
  82.2 6.5 %collective-permute-start.13 = (f32[5,1,32,256]{3,2,1,0:T(8,128)S(1)}, f32[5,1,32,256]{3,2,1,0:T(8,128)S(1)}, u32[]{:S(2)}, u32[]{:S(2)}) collective-permute-start(f32[5,1,32,256]{3,2,1,0:T(8,128)S(1)} %get-tuple-element.19), channel_id=1, source_target_pairs={{0,1},{1,2},{2,3},{3,4},{4,5},{5,6},{6,7},{7,8},{8,9},{9,10},{10,1... | collective-permute-start | bytes 491528 | tf_op jit(solution)/shard_map/ppermute | solution.py:18
  88.7 1.3 collective-permute-start.12
  90.0 1.9 collective-permute-done.12
  92.4 4.7 %copy.28 = f32[4,2,32,256]{0,3,2,1:T(8,128)} copy(f32[4,2,32,256]{3,2,1,0:T(8,128)S(1)} %get-tuple-element.15) | data formatting | bytes 524288 | tf_op jit(solution)/shard_map/slice | solution.py:89
  97.1 5.6 %scatter_custom_fusion.1 = f32[4,16384]{0,1:T(8,128)} fusion(s32[64]{0:T(128)S(1)} %get-tuple-element.14, f32[]{:T(128)} %constant.71.clone.1, f32[]{:T(128)} %constant.79.clone.1, f32[64]{0:T(128)S(1)} %copy-done.18, pred[64]{0:T(512)(128)(4,1)S(1)} %get-tuple-element.13, f32[4,16384]{0,1:T(8,128)} %bitcast.126, s32[1024]{0:T(1024)S(1)} %pad_clamp_fusion), kind=kCustom, calls=%fused_computation.27 | custom fusion | flops 768 | bytes 529416 | tf_op jit(solution)/shard_map/scatter-add | solution.py:38
  102.7 5.2 %copy.29 = f32[4,2,32,256]{3,2,1,0:T(8,128)S(1)} copy(f32[4,2,32,256]{0,3,2,1:T(8,128)} %bitcast.127) | data formatting | bytes 524288 | tf_op jit(solution)/shard_map/reshape | solution.py:38
  108.0 6.5 %collective-permute-start.15 = (f32[4,1,32,256]{3,2,1,0:T(8,128)S(1)}, f32[4,1,32,256]{3,2,1,0:T(8,128)S(1)}, u32[]{:S(2)}, u32[]{:S(2)}) collective-permute-start(f32[4,1,32,256]{3,2,1,0:T(8,128)S(1)} %get-tuple-element.41), channel_id=1, source_target_pairs={{0,1},{1,2},{2,3},{3,4},{4,5},{5,6},{6,7},{7,8},{8,9},{9,10},{10,1... | collective-permute-start | bytes 393224 | tf_op jit(solution)/shard_map/ppermute | solution.py:18
  114.5 1.3 collective-permute-start.14
  115.8 4.7 %copy.32 = f32[4,2,32,256]{0,3,2,1:T(8,128)} copy(f32[4,2,32,256]{3,2,1,0:T(8,128)S(1)} %get-tuple-element.16) | data formatting | bytes 524288 | tf_op jit(solution)/shard_map/slice | solution.py:89
  120.5 5.6 %scatter_custom_fusion.2 = f32[4,16384]{0,1:T(8,128)} fusion(s32[64]{0:T(128)S(1)} %get-tuple-element.14, f32[]{:T(128)} %constant.71.clone.1, f32[]{:T(128)} %constant.79.clone.1, f32[64]{0:T(128)S(1)} %copy-done.18, pred[64]{0:T(512)(128)(4,1)S(1)} %get-tuple-element.13, f32[4,16384]{0,1:T(8,128)} %bitcast.128, s32[1024]{0:T(1024)S(1)} %pad_clamp_fusion), kind=kCustom, calls=%fused_computation.25 | custom fusion | flops 768 | bytes 529416 | tf_op jit(solution)/shard_map/scatter-add | solution.py:38
  126.1 5.2 %copy.33 = f32[4,2,32,256]{3,2,1,0:T(8,128)S(1)} copy(f32[4,2,32,256]{0,3,2,1:T(8,128)} %bitcast.129) | data formatting | bytes 524288 | tf_op jit(solution)/shard_map/reshape | solution.py:38
  131.6 3.0 collective-permute-start.17
  134.6 1.5 collective-permute-start.16
  136.1 4.7 %copy.35 = f32[4,2,32,256]{0,3,2,1:T(8,128)} copy(f32[4,2,32,256]{3,2,1,0:T(8,128)S(1)} %get-tuple-element.17) | data formatting | bytes 524288 | tf_op jit(solution)/shard_map/slice | solution.py:89
  140.9 5.6 %scatter_custom_fusion.3 = f32[4,16384]{0,1:T(8,128)} fusion(s32[64]{0:T(128)S(1)} %get-tuple-element.14, f32[]{:T(128)} %constant.71.clone.1, f32[]{:T(128)} %constant.79.clone.1, f32[64]{0:T(128)S(1)} %copy-done.18, pred[64]{0:T(512)(128)(4,1)S(1)} %get-tuple-element.13, f32[4,16384]{0,1:T(8,128)} %bitcast.130, s32[1024]{0:T(1024)S(1)} %pad_clamp_fusion), kind=kCustom, calls=%fused_computation.23 | custom fusion | flops 768 | bytes 529416 | tf_op jit(solution)/shard_map/scatter-add | solution.py:38
  146.4 5.2 %copy.36 = f32[4,2,32,256]{3,2,1,0:T(8,128)S(1)} copy(f32[4,2,32,256]{0,3,2,1:T(8,128)} %bitcast.131) | data formatting | bytes 524288 | tf_op jit(solution)/shard_map/reshape | solution.py:38
  151.9 5.6 %collective-permute-start.19 = (f32[4,1,32,256]{3,2,1,0:T(8,128)S(1)}, f32[4,1,32,256]{3,2,1,0:T(8,128)}, u32[]{:S(2)}, u32[]{:S(2)}) collective-permute-start(f32[4,1,32,256]{3,2,1,0:T(8,128)S(1)} %get-tuple-element.37), channel_id=1, source_target_pairs={{0,1},{1,2},{2,3},{3,4},{4,5},{5,6},{6,7},{7,8},{8,9},{9,10},{10,1... | collective-permute-start | bytes 393224 | tf_op jit(solution)/shard_map/ppermute | solution.py:18
  157.6 1.3 collective-permute-start.18
  158.9 4.7 %copy.37 = f32[4,2,32,256]{0,3,2,1:T(8,128)} copy(f32[4,2,32,256]{3,2,1,0:T(8,128)S(1)} %slice.584) | data formatting | bytes 524288 | tf_op jit(solution)/shard_map/slice | solution.py:89
  163.6 5.6 %scatter_custom_fusion.4 = f32[4,16384]{0,1:T(8,128)} fusion(s32[64]{0:T(128)S(1)} %get-tuple-element.14, f32[]{:T(128)} %constant.71.clone.1, f32[]{:T(128)} %constant.79.clone.1, f32[64]{0:T(128)S(1)} %copy-done.18, pred[64]{0:T(512)(128)(4,1)S(1)} %get-tuple-element.13, f32[4,16384]{0,1:T(8,128)} %bitcast.132, s32[1024]{0:T(1024)S(1)} %pad_clamp_fusion), kind=kCustom, calls=%fused_computation.21 | custom fusion | flops 768 | bytes 529416 | tf_op jit(solution)/shard_map/scatter-add | solution.py:38
  169.2 5.2 %copy.38 = f32[4,2,32,256]{3,2,1,0:T(8,128)S(1)} copy(f32[4,2,32,256]{0,3,2,1:T(8,128)} %bitcast.133) | data formatting | bytes 524288 | tf_op jit(solution)/shard_map/reshape | solution.py:38
  174.5 1.2 broadcast_multiply_fusion.2
  175.7 4.3 %collective-permute-start.21 = (f32[4,1,32,256]{3,2,1,0:T(8,128)S(1)}, f32[4,1,32,256]{3,2,1,0:T(8,128)}, u32[]{:S(2)}, u32[]{:S(2)}) collective-permute-start(f32[4,1,32,256]{3,2,1,0:T(8,128)S(1)} %get-tuple-element.35), channel_id=1, source_target_pairs={{0,1},{1,2},{2,3},{3,4},{4,5},{5,6},{6,7},{7,8},{8,9},{9,10},{10,1... | collective-permute-start | bytes 393224 | tf_op jit(solution)/shard_map/ppermute | solution.py:18
  180.0 1.3 collective-permute-start.20
  181.3 4.7 %copy.39 = f32[4,2,32,256]{0,3,2,1:T(8,128)} copy(f32[4,2,32,256]{3,2,1,0:T(8,128)S(1)} %slice.587) | data formatting | bytes 524288 | tf_op jit(solution)/shard_map/slice | solution.py:89
  186.0 5.6 %scatter_custom_fusion.5 = f32[4,16384]{0,1:T(8,128)} fusion(s32[64]{0:T(128)S(1)} %get-tuple-element.14, f32[]{:T(128)} %constant.71.clone.1, f32[]{:T(128)} %constant.79.clone.1, f32[64]{0:T(128)S(1)} %copy-done.18, pred[64]{0:T(512)(128)(4,1)S(1)} %get-tuple-element.13, f32[4,16384]{0,1:T(8,128)} %bitcast.134, s32[1024]{0:T(1024)S(1)} %pad_clamp_fusion), kind=kCustom, calls=%fused_computation.19 | custom fusion | flops 768 | bytes 529416 | tf_op jit(solution)/shard_map/scatter-add | solution.py:38
  191.6 5.2 %copy.40 = f32[4,2,32,256]{3,2,1,0:T(8,128)S(1)} copy(f32[4,2,32,256]{0,3,2,1:T(8,128)} %bitcast.135) | data formatting | bytes 524288 | tf_op jit(solution)/shard_map/reshape | solution.py:38
  196.8 1.2 broadcast_multiply_fusion.1
  198.1 3.6 %collective-permute-start.23 = (f32[4,1,32,256]{3,2,1,0:T(8,128)S(1)}, f32[4,1,32,256]{3,2,1,0:T(8,128)S(1)}, u32[]{:S(2)}, u32[]{:S(2)}) collective-permute-start(f32[4,1,32,256]{3,2,1,0:T(8,128)S(1)} %get-tuple-element.33), channel_id=1, source_target_pairs={{0,1},{1,2},{2,3},{3,4},{4,5},{5,6},{6,7},{7,8},{8,9},{9,10},{10,1... | collective-permute-start | bytes 393224 | tf_op jit(solution)/shard_map/ppermute | solution.py:18
  201.7 1.3 collective-permute-start.22
  203.0 4.7 %copy.41 = f32[4,2,32,256]{0,3,2,1:T(8,128)} copy(f32[4,2,32,256]{3,2,1,0:T(8,128)S(1)} %slice.590) | data formatting | bytes 524288 | tf_op jit(solution)/shard_map/slice | solution.py:89
  207.8 5.6 %scatter_custom_fusion.6 = f32[4,16384]{0,1:T(8,128)} fusion(s32[64]{0:T(128)S(1)} %get-tuple-element.14, f32[]{:T(128)} %constant.71.clone.1, f32[]{:T(128)} %constant.79.clone.1, f32[64]{0:T(128)S(1)} %copy-done.18, pred[64]{0:T(512)(128)(4,1)S(1)} %get-tuple-element.13, f32[4,16384]{0,1:T(8,128)} %bitcast.136, s32[1024]{0:T(1024)S(1)} %pad_clamp_fusion), kind=kCustom, calls=%fused_computation.17 | custom fusion | flops 768 | bytes 529416 | tf_op jit(solution)/shard_map/scatter-add | solution.py:38
  213.3 5.2 %copy.42 = f32[4,2,32,256]{3,2,1,0:T(8,128)S(1)} copy(f32[4,2,32,256]{0,3,2,1:T(8,128)} %bitcast.137) | data formatting | bytes 524288 | tf_op jit(solution)/shard_map/reshape | solution.py:38
  221.1 4.3 %collective-permute-start.25 = (f32[4,1,32,256]{3,2,1,0:T(8,128)S(1)}, f32[4,1,32,256]{3,2,1,0:T(8,128)S(1)}, u32[]{:S(2)}, u32[]{:S(2)}) collective-permute-start(f32[4,1,32,256]{3,2,1,0:T(8,128)S(1)} %get-tuple-element.31), channel_id=1, source_target_pairs={{0,1},{1,2},{2,3},{3,4},{4,5},{5,6},{6,7},{7,8},{8,9},{9,10},{10,1... | collective-permute-start | bytes 393224 | tf_op jit(solution)/shard_map/ppermute | solution.py:18
  225.4 1.5 collective-permute-start.24
  226.9 4.7 %copy.43 = f32[4,2,32,256]{0,3,2,1:T(8,128)} copy(f32[4,2,32,256]{3,2,1,0:T(8,128)S(1)} %slice.593) | data formatting | bytes 524288 | tf_op jit(solution)/shard_map/slice | solution.py:89
  231.7 5.6 %scatter_custom_fusion.7 = f32[4,16384]{0,1:T(8,128)} fusion(s32[64]{0:T(128)S(1)} %get-tuple-element.14, f32[]{:T(128)} %constant.71.clone.1, f32[]{:T(128)} %constant.79.clone.1, f32[64]{0:T(128)S(1)} %copy-done.18, pred[64]{0:T(512)(128)(4,1)S(1)} %get-tuple-element.13, f32[4,16384]{0,1:T(8,128)} %bitcast.124, s32[1024]{0:T(1024)S(1)} %pad_clamp_fusion), kind=kCustom, calls=%fused_computation.15 | custom fusion | flops 768 | bytes 529416 | tf_op jit(solution)/shard_map/scatter-add | solution.py:38
  237.3 5.3 %copy.44 = f32[4,2,32,256]{3,2,1,0:T(8,128)S(1)} copy(f32[4,2,32,256]{0,3,2,1:T(8,128)} %bitcast.125) | data formatting | bytes 524288 | tf_op jit(solution)/shard_map/reshape | solution.py:38
  244.0 45.1 %all-gather.4.cloned.1.call-done = f32[4,4,16384]{2,1,0:T(4,128)} async-done(((f32[1,4,16384]{2,1,0:T(4,128)}), f32[4,4,16384]{2,1,0:T(4,128)}) %all-gather.4.cloned.1.call-update) | async-done | bytes 1048592 | tf_op jit(solution)/shard_map/all_gather | solution.py:103
  289.0 1.6 reshape.326
  290.6 1.5 fusion.185
  292.1 51.3 %all-gather = f32[1024,16]{1,0:T(8,128)S(1)} all-gather(f32[16,16]{1,0:T(8,128)S(1)} %fusion.185), channel_id=2, replica_groups=mesh['probe'=4,'space'=64] {'space'}, dimensions={0}, use_global_device_ids=true | all-gather | bytes 66560 | tf_op jit(solution)/shard_map/all_gather | solution.py:8
  343.6 1.5 cholesky.16
  346.4 1.2 custom-call.6
  (134 shorter events, 22.0 us)
Async XLA Ops:
  7.2 40.4 %copy-start = (f32[2,32,256]{2,1,0:T(8,128)S(1)}, f32[2,32,256]{2,1,0:T(8,128)}, u32[]{:S(2)}) copy-start(f32[2,32,256]{2,1,0:T(8,128)} %param.10) | copy-start | bytes 196612
  7.2 41.0 %copy-start.1 = (f32[4,2,32,256]{3,2,1,0:T(8,128)S(1)}, f32[4,2,32,256]{3,2,1,0:T(8,128)}, u32[]{:S(2)}) copy-start(f32[4,2,32,256]{3,2,1,0:T(8,128)} %param.11) | copy-start | bytes 786436
  7.2 281.8 %all-gather.4.cloned.1.call-start = ((), (), s32[]{:S(2)}) async-start(), calls=%async_computation | async-start | bytes 1310720 | tf_op jit(solution)/shard_map/all_gather | solution.py:103
  15.6 3.1 collective-permute-start.1
  17.4 5.0 %collective-permute-start = (f32[5,1,32,256]{3,2,1,0:T(8,128)S(1)}, f32[5,1,32,256]{3,2,1,0:T(8,128)S(1)}, u32[]{:S(2)}, u32[]{:S(2)}) collective-permute-start(f32[5,1,32,256]{3,2,1,0:T(8,128)S(1)} %get-tuple-element.50), channel_id=1, source_target_pairs={{1,0},{2,1},{3,2},{4,3},{5,4},{6,5},{7,6},{8,7},{9,8},{10,9},{11,1... | collective-permute-start | bytes 491528 | tf_op jit(solution)/shard_map/ppermute | solution.py:21
  25.6 7.1 %collective-permute-start.3 = (f32[5,1,32,256]{3,2,1,0:T(8,128)S(1)}, f32[5,1,32,256]{3,2,1,0:T(8,128)S(1)}, u32[]{:S(2)}, u32[]{:S(2)}) collective-permute-start(f32[5,1,32,256]{3,2,1,0:T(8,128)S(1)} %get-tuple-element.29), channel_id=1, source_target_pairs={{0,1},{1,2},{2,3},{3,4},{4,5},{5,6},{6,7},{7,8},{8,9},{9,10},{10,1... | collective-permute-start | bytes 491528 | tf_op jit(solution)/shard_map/ppermute | solution.py:18
  31.3 3.3 collective-permute-start.2
  35.7 0.6 copy-start.3
  38.5 6.9 %collective-permute-start.5 = (f32[5,1,32,256]{3,2,1,0:T(8,128)S(1)}, f32[5,1,32,256]{3,2,1,0:T(8,128)S(1)}, u32[]{:S(2)}, u32[]{:S(2)}) collective-permute-start(f32[5,1,32,256]{3,2,1,0:T(8,128)S(1)} %get-tuple-element.27), channel_id=1, source_target_pairs={{0,1},{1,2},{2,3},{3,4},{4,5},{5,6},{6,7},{7,8},{8,9},{9,10},{10,1... | collective-permute-start | bytes 491528 | tf_op jit(solution)/shard_map/ppermute | solution.py:18
  44.0 3.3 collective-permute-start.4
  45.4 44.6 %copy-start.19 = (s32[64]{0:T(128)S(1)}, s32[64]{0:T(128)}, u32[]{:S(2)}) copy-start(s32[64]{0:T(128)} %param.16) | copy-start | bytes 772
  47.6 0.6 copy-start.5
  48.6 6.9 %collective-permute-start.7 = (f32[5,1,32,256]{3,2,1,0:T(8,128)S(1)}, f32[5,1,32,256]{3,2,1,0:T(8,128)S(1)}, u32[]{:S(2)}, u32[]{:S(2)}) collective-permute-start(f32[5,1,32,256]{3,2,1,0:T(8,128)S(1)} %get-tuple-element.25), channel_id=1, source_target_pairs={{0,1},{1,2},{2,3},{3,4},{4,5},{5,6},{6,7},{7,8},{8,9},{9,10},{10,1... | collective-permute-start | bytes 491528 | tf_op jit(solution)/shard_map/ppermute | solution.py:18
  54.1 3.3 collective-permute-start.6
  57.7 0.6 copy-start.7
  58.6 9.3 %collective-permute-start.9 = (f32[5,1,32,256]{3,2,1,0:T(8,128)S(1)}, f32[5,1,32,256]{3,2,1,0:T(8,128)S(1)}, u32[]{:S(2)}, u32[]{:S(2)}) collective-permute-start(f32[5,1,32,256]{3,2,1,0:T(8,128)S(1)} %get-tuple-element.23), channel_id=1, source_target_pairs={{0,1},{1,2},{2,3},{3,4},{4,5},{5,6},{6,7},{7,8},{8,9},{9,10},{10,1... | collective-permute-start | bytes 491528 | tf_op jit(solution)/shard_map/ppermute | solution.py:18
  66.6 3.3 collective-permute-start.8
  70.2 0.6 copy-start.9
  71.2 7.8 %collective-permute-start.11 = (f32[5,1,32,256]{3,2,1,0:T(8,128)S(1)}, f32[5,1,32,256]{3,2,1,0:T(8,128)S(1)}, u32[]{:S(2)}, u32[]{:S(2)}) collective-permute-start(f32[5,1,32,256]{3,2,1,0:T(8,128)S(1)} %get-tuple-element.21), channel_id=1, source_target_pairs={{0,1},{1,2},{2,3},{3,4},{4,5},{5,6},{6,7},{7,8},{8,9},{9,10},{10,1... | collective-permute-start | bytes 491528 | tf_op jit(solution)/shard_map/ppermute | solution.py:18
  77.6 3.3 collective-permute-start.10
  78.9 18.2 %copy-start.18 = (f32[64]{0:T(128)S(1)}, f32[64]{0:T(128)}, u32[]{:S(2)}) copy-start(f32[64]{0:T(128)} %param.17) | copy-start | bytes 772
  81.2 0.6 copy-start.11
  82.2 7.9 %collective-permute-start.13 = (f32[5,1,32,256]{3,2,1,0:T(8,128)S(1)}, f32[5,1,32,256]{3,2,1,0:T(8,128)S(1)}, u32[]{:S(2)}, u32[]{:S(2)}) collective-permute-start(f32[5,1,32,256]{3,2,1,0:T(8,128)S(1)} %get-tuple-element.19), channel_id=1, source_target_pairs={{0,1},{1,2},{2,3},{3,4},{4,5},{5,6},{6,7},{7,8},{8,9},{9,10},{10,1... | collective-permute-start | bytes 491528 | tf_op jit(solution)/shard_map/ppermute | solution.py:18
  88.7 3.3 collective-permute-start.12
  92.2 10.4 %copy-start.13 = (f32[2,32,256]{2,1,0:T(8,128)}, f32[2,32,256]{2,1,0:T(8,128)S(1)}, u32[]{:S(2)}) copy-start(f32[2,32,256]{2,1,0:T(8,128)S(1)} %fusion.112) | copy-start | bytes 196612
  108.0 23.3 %collective-permute-start.15 = (f32[4,1,32,256]{3,2,1,0:T(8,128)S(1)}, f32[4,1,32,256]{3,2,1,0:T(8,128)S(1)}, u32[]{:S(2)}, u32[]{:S(2)}) collective-permute-start(f32[4,1,32,256]{3,2,1,0:T(8,128)S(1)} %get-tuple-element.41), channel_id=1, source_target_pairs={{0,1},{1,2},{2,3},{3,4},{4,5},{5,6},{6,7},{7,8},{8,9},{9,10},{10,1... | collective-permute-start | bytes 393224 | tf_op jit(solution)/shard_map/ppermute | solution.py:18
  114.5 16.9 %collective-permute-start.14 = (f32[4,1,32,256]{3,2,1,0:T(8,128)S(1)}, f32[4,1,32,256]{3,2,1,0:T(8,128)S(1)}, u32[]{:S(2)}, u32[]{:S(2)}) collective-permute-start(f32[4,1,32,256]{3,2,1,0:T(8,128)S(1)} %get-tuple-element.40), channel_id=1, source_target_pairs={{1,0},{2,1},{3,2},{4,3},{5,4},{6,5},{7,6},{8,7},{9,8},{10,9},{11,1... | collective-permute-start | bytes 393224 | tf_op jit(solution)/shard_map/ppermute | solution.py:21
  131.6 20.1 %collective-permute-start.17 = (f32[4,1,32,256]{3,2,1,0:T(8,128)S(1)}, f32[4,1,32,256]{3,2,1,0:T(8,128)S(1)}, u32[]{:S(2)}, u32[]{:S(2)}) collective-permute-start(f32[4,1,32,256]{3,2,1,0:T(8,128)S(1)} %get-tuple-element.39), channel_id=1, source_target_pairs={{0,1},{1,2},{2,3},{3,4},{4,5},{5,6},{6,7},{7,8},{8,9},{9,10},{10,1... | collective-permute-start | bytes 393224 | tf_op jit(solution)/shard_map/ppermute | solution.py:18
  134.6 17.0 %collective-permute-start.16 = (f32[4,1,32,256]{3,2,1,0:T(8,128)S(1)}, f32[4,1,32,256]{3,2,1,0:T(8,128)S(1)}, u32[]{:S(2)}, u32[]{:S(2)}) collective-permute-start(f32[4,1,32,256]{3,2,1,0:T(8,128)S(1)} %get-tuple-element.38), channel_id=1, source_target_pairs={{1,0},{2,1},{3,2},{4,3},{5,4},{6,5},{7,6},{8,7},{9,8},{10,9},{11,1... | collective-permute-start | bytes 393224 | tf_op jit(solution)/shard_map/ppermute | solution.py:21
  151.9 22.5 %collective-permute-start.19 = (f32[4,1,32,256]{3,2,1,0:T(8,128)S(1)}, f32[4,1,32,256]{3,2,1,0:T(8,128)}, u32[]{:S(2)}, u32[]{:S(2)}) collective-permute-start(f32[4,1,32,256]{3,2,1,0:T(8,128)S(1)} %get-tuple-element.37), channel_id=1, source_target_pairs={{0,1},{1,2},{2,3},{3,4},{4,5},{5,6},{6,7},{7,8},{8,9},{9,10},{10,1... | collective-permute-start | bytes 393224 | tf_op jit(solution)/shard_map/ppermute | solution.py:18
  157.6 16.9 %collective-permute-start.18 = (f32[4,1,32,256]{3,2,1,0:T(8,128)S(1)}, f32[4,1,32,256]{3,2,1,0:T(8,128)}, u32[]{:S(2)}, u32[]{:S(2)}) collective-permute-start(f32[4,1,32,256]{3,2,1,0:T(8,128)S(1)} %get-tuple-element.36), channel_id=1, source_target_pairs={{1,0},{2,1},{3,2},{4,3},{5,4},{6,5},{7,6},{8,7},{9,8},{10,9},{11,1... | collective-permute-start | bytes 393224 | tf_op jit(solution)/shard_map/ppermute | solution.py:21
  175.7 21.1 %collective-permute-start.21 = (f32[4,1,32,256]{3,2,1,0:T(8,128)S(1)}, f32[4,1,32,256]{3,2,1,0:T(8,128)}, u32[]{:S(2)}, u32[]{:S(2)}) collective-permute-start(f32[4,1,32,256]{3,2,1,0:T(8,128)S(1)} %get-tuple-element.35), channel_id=1, source_target_pairs={{0,1},{1,2},{2,3},{3,4},{4,5},{5,6},{6,7},{7,8},{8,9},{9,10},{10,1... | collective-permute-start | bytes 393224 | tf_op jit(solution)/shard_map/ppermute | solution.py:18
  180.0 16.9 %collective-permute-start.20 = (f32[4,1,32,256]{3,2,1,0:T(8,128)S(1)}, f32[4,1,32,256]{3,2,1,0:T(8,128)}, u32[]{:S(2)}, u32[]{:S(2)}) collective-permute-start(f32[4,1,32,256]{3,2,1,0:T(8,128)S(1)} %get-tuple-element.34), channel_id=1, source_target_pairs={{1,0},{2,1},{3,2},{4,3},{5,4},{6,5},{7,6},{8,7},{9,8},{10,9},{11,1... | collective-permute-start | bytes 393224 | tf_op jit(solution)/shard_map/ppermute | solution.py:21
  198.1 20.5 %collective-permute-start.23 = (f32[4,1,32,256]{3,2,1,0:T(8,128)S(1)}, f32[4,1,32,256]{3,2,1,0:T(8,128)S(1)}, u32[]{:S(2)}, u32[]{:S(2)}) collective-permute-start(f32[4,1,32,256]{3,2,1,0:T(8,128)S(1)} %get-tuple-element.33), channel_id=1, source_target_pairs={{0,1},{1,2},{2,3},{3,4},{4,5},{5,6},{6,7},{7,8},{8,9},{9,10},{10,1... | collective-permute-start | bytes 393224 | tf_op jit(solution)/shard_map/ppermute | solution.py:18
  201.7 16.9 %collective-permute-start.22 = (f32[4,1,32,256]{3,2,1,0:T(8,128)S(1)}, f32[4,1,32,256]{3,2,1,0:T(8,128)S(1)}, u32[]{:S(2)}, u32[]{:S(2)}) collective-permute-start(f32[4,1,32,256]{3,2,1,0:T(8,128)S(1)} %get-tuple-element.32), channel_id=1, source_target_pairs={{1,0},{2,1},{3,2},{4,3},{5,4},{6,5},{7,6},{8,7},{9,8},{10,9},{11,1... | collective-permute-start | bytes 393224 | tf_op jit(solution)/shard_map/ppermute | solution.py:21
  218.6 0.7 copy-start.15
  219.2 0.7 copy-start.16
  221.1 21.5 %collective-permute-start.25 = (f32[4,1,32,256]{3,2,1,0:T(8,128)S(1)}, f32[4,1,32,256]{3,2,1,0:T(8,128)S(1)}, u32[]{:S(2)}, u32[]{:S(2)}) collective-permute-start(f32[4,1,32,256]{3,2,1,0:T(8,128)S(1)} %get-tuple-element.31), channel_id=1, source_target_pairs={{0,1},{1,2},{2,3},{3,4},{4,5},{5,6},{6,7},{7,8},{8,9},{9,10},{10,1... | collective-permute-start | bytes 393224 | tf_op jit(solution)/shard_map/ppermute | solution.py:18
  225.4 17.2 %collective-permute-start.24 = (f32[4,1,32,256]{3,2,1,0:T(8,128)S(1)}, f32[4,1,32,256]{3,2,1,0:T(8,128)S(1)}, u32[]{:S(2)}, u32[]{:S(2)}) collective-permute-start(f32[4,1,32,256]{3,2,1,0:T(8,128)S(1)} %get-tuple-element.30), channel_id=1, source_target_pairs={{1,0},{2,1},{3,2},{4,3},{5,4},{6,5},{7,6},{8,7},{9,8},{10,9},{11,1... | collective-permute-start | bytes 393224 | tf_op jit(solution)/shard_map/ppermute | solution.py:21
  237.2 5.4 %copy-start.4 = (f32[2,32,256]{2,1,0:T(8,128)S(1)}, f32[2,32,256]{2,1,0:T(8,128)}, u32[]{:S(2)}) copy-start(f32[2,32,256]{2,1,0:T(8,128)} %copy-done.3) | copy-start | bytes 196612
  237.2 5.4 %copy-start.6 = (f32[2,32,256]{2,1,0:T(8,128)S(1)}, f32[2,32,256]{2,1,0:T(8,128)}, u32[]{:S(2)}) copy-start(f32[2,32,256]{2,1,0:T(8,128)} %copy-done.5) | copy-start | bytes 196612
  237.2 5.4 %copy-start.8 = (f32[2,32,256]{2,1,0:T(8,128)S(1)}, f32[2,32,256]{2,1,0:T(8,128)}, u32[]{:S(2)}) copy-start(f32[2,32,256]{2,1,0:T(8,128)} %copy-done.7) | copy-start | bytes 196612
  237.2 5.4 %copy-start.10 = (f32[2,32,256]{2,1,0:T(8,128)S(1)}, f32[2,32,256]{2,1,0:T(8,128)}, u32[]{:S(2)}) copy-start(f32[2,32,256]{2,1,0:T(8,128)} %copy-done.9) | copy-start | bytes 196612
  237.2 5.4 %copy-start.12 = (f32[2,32,256]{2,1,0:T(8,128)S(1)}, f32[2,32,256]{2,1,0:T(8,128)}, u32[]{:S(2)}) copy-start(f32[2,32,256]{2,1,0:T(8,128)} %copy-done.11) | copy-start | bytes 196612
  237.3 5.4 %copy-start.14 = (f32[2,32,256]{2,1,0:T(8,128)S(1)}, f32[2,32,256]{2,1,0:T(8,128)}, u32[]{:S(2)}) copy-start(f32[2,32,256]{2,1,0:T(8,128)} %copy-done.13) | copy-start | bytes 196612
  237.3 5.4 %copy-start.17 = (f32[2,32,256]{2,1,0:T(8,128)S(1)}, f32[2,32,256]{2,1,0:T(8,128)}, u32[]{:S(2)}) copy-start(f32[2,32,256]{2,1,0:T(8,128)} %param.12) | copy-start | bytes 196612
  243.1 106.4 %copy-start.2 = (f32[4,2,32,256]{3,2,1,0:T(8,128)}, f32[4,2,32,256]{3,2,1,0:T(8,128)S(1)}, u32[]{:S(2)}) copy-start(f32[4,2,32,256]{3,2,1,0:T(8,128)S(1)} %fusion.103) | copy-start | bytes 786436
Sparse Core Ops, SparseCore 0:
  244.1 44.8 all-gather.3
